TPU v7x, 512 devices: a whole 4x4x16 slice. The times are simulated.
512 devices in a mesh: dst: 32 (over z, core), src: 16 (over y, x).
Axes of the slice: x: 4, y: 4, z: 16, core: 2. Of those that a mesh axis runs over, the one named last changes fastest.
Arguments:
- adj_tiles: bfloat16 [32, 16, 64, 64, 512], P('dst', 'src'), may hold values from 0 to 0.011047363
- tile_cols: int32 [32, 16, 64, 8], P('dst', 'src'), may hold values from 0 to 63
- send_block: int32 [32, 16, 32, 2], P('dst', 'src'), may hold values from 0 to 15
- send_count: int32 [32, 16, 32], P('dst', 'src'), may hold values from 1 to 2, as said below
- history: bfloat16 [64, 16, 8192], P('dst', 'src'), may hold values from -6 to 6
- node_feats: bfloat16 [512, 8192], P('dst', 'src'), may hold values from -6 to 6
- w_neigh: bfloat16 [128, 128], replicated, may hold values from -0.5 to 0.5
- w_self: bfloat16 [128, 128], replicated, may hold values from -0.5 to 0.5
- out_bias: float32 [128], replicated, may hold values from -3 to 3
- cotangent: bfloat16 [512, 8192], P('dst', 'src'), may hold values from -6 to 6
Outputs:
- new_embed: bfloat16 [512, 8192], P('dst', 'src')
- grad_neigh: float32 [128, 128], replicated
- grad_self: float32 [128, 128], replicated
- grad_bias: float32 [128], replicated
Inputs may be any that keep to these rules, and one draw needn't show every extreme that they name: `send_count`: in every draw, for each source group some owner gets 2 live slots from every device of that group.
All inputs are finite; a program needn't handle non-finite values.
Results may differ from a plain program's by a relative error of at most 0.0052.
Values may be sent and summed in bfloat16 or wider, within the bound.
A program may use at most 64 MiB of HBM per device.

v0:
```python
import jax
import jax.numpy as jnp
from jax import lax
from jax.sharding import PartitionSpec as P


def on_device(
    adj_tiles,
    tile_cols,
    send_block,
    send_count,
    history,
    node_feats,
    w_neigh,
    w_self,
    out_bias,
    cotangent,
):
    owners = lax.axis_size("dst")
    groups = lax.axis_size("src")
    slot_count = adj_tiles.shape[2]
    block_size = adj_tiles.shape[3]
    feat_width = w_neigh.shape[0]
    capacity = slot_count // owners
    own_blocks = node_feats.shape[0]
    gathered = lax.all_gather(history, "dst", axis=0, tiled=True)
    group_table = gathered.reshape(-1, block_size, feat_width)
    picked = group_table[tile_cols.reshape(-1)].reshape(slot_count, -1, feat_width)
    tiles_flat = adj_tiles.reshape(slot_count, block_size, -1)
    partial_value = jnp.einsum(
        "sir,srf->sif", tiles_flat, picked, preferred_element_type=jnp.float32
    )
    alive_mask = (jnp.arange(capacity)[None, :] < send_count.reshape(owners, 1)).astype(jnp.float32)
    partial_value = (
        partial_value.reshape(owners, capacity, block_size * feat_width) * alive_mask[:, :, None]
    )
    targets = send_block.reshape(owners, capacity)
    spread = jnp.broadcast_to(targets[:, :, None], (owners, capacity, groups))
    arrived, arrived_ids = (
        lax.all_to_all(
            lax.all_to_all(partial_value, "dst", split_axis=0, concat_axis=0, tiled=True),
            "src",
            split_axis=2,
            concat_axis=1,
            tiled=True,
        ),
        lax.all_to_all(
            lax.all_to_all(spread, "dst", split_axis=0, concat_axis=0, tiled=True),
            "src",
            split_axis=2,
            concat_axis=1,
            tiled=True,
        ),
    )
    selector = (arrived_ids.reshape(1, -1) == jnp.arange(own_blocks)[:, None]).astype(jnp.float32)
    summed = jnp.dot(
        selector,
        arrived.reshape(selector.shape[1], -1),
        precision=lax.Precision.HIGHEST,
        preferred_element_type=jnp.float32,
    )
    agg_rows = summed.astype(jnp.bfloat16).reshape(-1, feat_width)
    self_rows = node_feats.reshape(-1, feat_width)
    pre_act = (
        jnp.dot(agg_rows, w_neigh, preferred_element_type=jnp.float32)
        + jnp.dot(self_rows, w_self, preferred_element_type=jnp.float32)
        + out_bias
    )
    sigmoid_z = jax.nn.sigmoid(pre_act)
    new_embed = (pre_act * sigmoid_z).astype(jnp.bfloat16).reshape(node_feats.shape)
    loss_scale = float(own_blocks * owners * block_size) ** (-0.5)
    slope = sigmoid_z * (1.0 + pre_act * (1.0 - sigmoid_z))
    grad_pre = cotangent.reshape(-1, feat_width).astype(jnp.float32) * slope * loss_scale
    grad_low = grad_pre.astype(jnp.bfloat16)
    grad_neigh = jnp.dot(agg_rows.T, grad_low, preferred_element_type=jnp.float32)
    grad_self = jnp.dot(self_rows.T, grad_low, preferred_element_type=jnp.float32)
    grad_bias = jnp.sum(grad_pre, axis=0)
    grad_neigh, grad_self, grad_bias = lax.psum((grad_neigh, grad_self, grad_bias), ("dst", "src"))
    return (new_embed, grad_neigh, grad_self, grad_bias)


def solution(mesh):
    in_specs = (
        P("dst", "src", None, None, None),
        P("dst", "src", None, None),
        P("dst", "src", None, None),
        P("dst", "src", None),
        P("dst", "src", None),
        P("dst", "src"),
        P(),
        P(),
        P(),
        P("dst", "src"),
    )
    out_specs = (P("dst", "src"), P(), P(), P())
    return jax.shard_map(
        on_device, mesh=mesh, in_specs=in_specs, out_specs=out_specs, check_vma=False
    )
```

profile of v0, /device:TPU:1, one launch (start us, length us, event | category | flops | bytes accessed | tf_op | source)
XLA Modules:
  0.0 780.6 jit_solution(10505770939572856301)
XLA Ops:
  7.2 1.4 copy.38
  8.7 0.8 copy.35
  9.5 0.7 broadcast_in_dim.5
  10.2 16.8 %all-to-all-start = ((s32[32,2,16]{2,1,0:T(2,128)}), s32[32,2,16]{2,1,0:T(2,128)S(1)}, u32[]{:S(2)}, u32[]{:S(2)}) async-start(s32[32,2,16]{2,1,0:T(2,128)} %broadcast_in_dim.5), calls=%async_computation | async-start | bytes 65536 | tf_op jit(solution)/shard_map/all_to_all | solution.py:48
  26.9 0.8 copy.39
  27.8 0.7 fusion.7
  28.5 59.7 %all-gather.2.cloned.1.call-done = bf16[64,1,8192]{2,1,0:T(2,128)(2,1)} async-done(((bf16[2,1,8192]{2,1,0:T(2,128)(2,1)}), bf16[64,1,8192]{2,1,0:T(2,128)(2,1)}) %all-gather.2.cloned.1.call-update) | async-done | bytes 1048592 | tf_op jit(solution)/shard_map/all_gather | solution.py:26
  88.3 7.9 %reduce = bf16[64,8192]{1,0:T(8,128)(2,1)S(1)} reduce(bf16[64,1,8192]{2,1,0:T(2,128)(2,1)} %all-gather.2.cloned.1.call-done, bf16[]{:T(256)} %constant.17), dimensions={1}, to_apply=%all_gather.3.reduce_sub_computation | reduce | bytes 2097154 | tf_op jit(solution)/shard_map/all_gather | solution.py:26
  96.4 13.5 %gather_fusion = bf16[512,64,128]{2,1,0:T(8,128)(2,1)} fusion(bf16[64,64,128]{2,1,0:T(8,128)(2,1)S(1)} %bitcast.38, s32[1024]{0:T(1024)S(1)} %pad_clamp_fusion), kind=kCustom, calls=%fused_computation | custom fusion | bytes 16779264 | tf_op jit(solution)/shard_map/gather | solution.py:28
  109.9 6.3 fusion.2
  116.3 2.2 reshape.102
  118.5 4.2 broadcast_multiply_fusion
  122.7 8.2 %all-to-all-start.2 = ((f32[32,2,8192]{2,1,0:T(2,128)}), f32[32,2,8192]{2,1,0:T(2,128)S(1)}, u32[]{:S(2)}, u32[]{:S(2)}) async-start(f32[32,2,8192]{2,1,0:T(2,128)} %broadcast_multiply_fusion), calls=%async_computation.2 | async-start | bytes 4194304 | tf_op jit(solution)/shard_map/all_to_all | solution.py:41
  131.0 0.7 copy.36
  131.6 97.9 %all-to-all-done.2 = f32[32,2,8192]{2,1,0:T(2,128)S(1)} async-done(((f32[32,2,8192]{2,1,0:T(2,128)}), f32[32,2,8192]{2,1,0:T(2,128)S(1)}, u32[]{:S(2)}, u32[]{:S(2)}) %all-to-all-start.2) | async-done | bytes 2097184 | tf_op jit(solution)/shard_map/all_to_all | solution.py:41
  229.6 6.4 all-to-all-start.1
  236.0 8.6 %copy.40 = f32[32,2,8192]{0,1,2:T(2,128)} copy(f32[32,2,8192]{2,1,0:T(2,128)S(1)} %all-to-all-done.2) | data formatting | bytes 4194304 | tf_op jit(solution)/shard_map/all_to_all | solution.py:41
  244.6 11.4 %reshape.117 = f32[16,1,32768]{2,1,0:T(1,128)} reshape(f32[8192,2,32]{2,1,0:T(2,128)} %bitcast.40) | data formatting | bytes 4194304
  256.0 6.8 all-to-all-start.3
  263.3 27.6 %all-to-all-done.3 = f32[16,1,32768]{2,1,0:T(1,128)S(1)} async-done(((f32[16,1,32768]{2,1,0:T(1,128)}), f32[16,1,32768]{2,1,0:T(1,128)S(1)}, u32[]{:S(2)}, u32[]{:S(2)}) %all-to-all-start.3) | async-done | bytes 2097184 | tf_op jit(solution)/shard_map/all_to_all | solution.py:40
  290.9 1.3 copy-done.1
  292.8 7.3 reduce.1
  300.1 9.2 %reshape.118 = f32[8192,2,32]{2,1,0:T(2,128)} reshape(f32[16,32768]{1,0:T(8,128)S(1)} %reduce.1) | data formatting | bytes 4194304
  309.3 10.3 %copy.41 = f32[32,2,16,512]{3,1,2,0:T(2,128)S(1)} copy(f32[32,2,16,512]{0,1,3,2:T(2,128)} %bitcast.41) | data formatting | bytes 4194304 | tf_op jit(solution)/shard_map/all_to_all | solution.py:40
  319.6 2.5 reshape.103
  322.1 2.4 convolution_convert_fusion
  324.9 0.8 convolution_bitcast_fusion
  325.7 0.8 fusion.9
  327.2 103.9 %psum.23 = f32[128]{0:T(128)} all-reduce(f32[128]{0:T(128)S(1)} %get-tuple-element.26), channel_id=1, replica_groups=mesh['dst'=32,'src'=16] {'dst','src'}, use_global_device_ids=true, to_apply=%region_3.0 | all-reduce | flops 128 | bytes 1024 | tf_op jit(solution)/shard_map/psum | solution.py:78
  431.1 339.6 %all-reduce.3.cloned.1.call-done = (f32[128,128]{1,0:T(8,128)}, f32[128,128]{0,1:T(8,128)}) async-done(((f32[128,128]{1,0:T(8,128)}, f32[128,128]{0,1:T(8,128)}), (f32[128,128]{1,0:T(8,128)}, f32[128,128]{0,1:T(8,128)})) %all-reduce.3.cloned.1.call-update) | async-done | bytes 131088 | tf_op jit(solution)/shard_map/psum | solution.py:78
  770.7 1.6 copy.42
  772.3 1.5 copy.46
  (30 shorter events, 2.4 us)
Async XLA Ops:
  7.2 317.5 %copy-start = (bf16[128,128]{1,0:T(8,128)(2,1)S(1)}, bf16[128,128]{1,0:T(8,128)(2,1)}, u32[]{:S(2)}) copy-start(bf16[128,128]{1,0:T(8,128)(2,1)} %param.17) | copy-start | bytes 98308
  7.2 81.1 %all-gather.2.cloned.1.call-start = ((), (), s32[]{:S(2)}) async-start(), calls=%async_computation.4 | async-start | bytes 2162688 | tf_op jit(solution)/shard_map/all_gather | solution.py:26
  10.2 112.5 %all-to-all-start = ((s32[32,2,16]{2,1,0:T(2,128)}), s32[32,2,16]{2,1,0:T(2,128)S(1)}, u32[]{:S(2)}, u32[]{:S(2)}) async-start(s32[32,2,16]{2,1,0:T(2,128)} %broadcast_in_dim.5), calls=%async_computation | async-start | bytes 65536 | tf_op jit(solution)/shard_map/all_to_all | solution.py:48
  122.7 106.8 %all-to-all-start.2 = ((f32[32,2,8192]{2,1,0:T(2,128)}), f32[32,2,8192]{2,1,0:T(2,128)S(1)}, u32[]{:S(2)}, u32[]{:S(2)}) async-start(f32[32,2,8192]{2,1,0:T(2,128)} %broadcast_multiply_fusion), calls=%async_computation.2 | async-start | bytes 4194304 | tf_op jit(solution)/shard_map/all_to_all | solution.py:41
  229.6 26.4 %all-to-all-start.1 = ((s32[32,2,16]{0,1,2:T(2,128)}), s32[32,2,16]{0,1,2:T(2,128)S(1)}, u32[]{:S(2)}, u32[]{:S(2)}) async-start(s32[32,2,16]{0,1,2:T(2,128)} %copy.36), calls=%async_computation.1 | async-start | bytes 32768 | tf_op jit(solution)/shard_map/all_to_all | solution.py:47
  256.0 6.9 copy-start.4
  256.0 6.9 copy-start.3
  256.0 34.9 %all-to-all-start.3 = ((f32[16,1,32768]{2,1,0:T(1,128)}), f32[16,1,32768]{2,1,0:T(1,128)S(1)}, u32[]{:S(2)}, u32[]{:S(2)}) async-start(f32[16,1,32768]{2,1,0:T(1,128)} %reshape.117), calls=%async_computation.3 | async-start | bytes 4194304 | tf_op jit(solution)/shard_map/all_to_all | solution.py:40
  262.8 507.9 %all-reduce.3.cloned.1.call-start = ((), (), s32[]{:S(2)}) async-start(), calls=%async_computation.5 | async-start | bytes 262144 | tf_op jit(solution)/shard_map/psum | solution.py:78
  290.9 1.3 copy-start.1
  322.1 2.4 copy-start.2
  322.1 2.6 copy-start.5
Sparse Core Ops, SparseCore 0:
  10.7 77.5 all-gather.1
  326.7 444.0 all-reduce.2
where the time goes:
time: 782 us; the launch traced here: 781 us
  waiting for transfers between devices  525 us (67%)
  blocking collectives  104 us (13%)
  local copies, waits for them, and re-layouts  68.5 us (9%)
  starting transfers between devices  38.3 us (5%)
  other arithmetic  20.1 us (3%)
  between operations  14.2 us (2%)
  matrix products  10.7 us (1%)
    psum x1, waiting for transfers between devices, on_device(): lax.psum((grad_neigh, grad_self, grad_bias), ('dst', 'src'))  340 us
    psum x1, blocking collectives, on_device(): lax.psum((grad_neigh, grad_self, grad_bias), ('dst', 'src'))  104 us
    all_to_all x1, waiting for transfers between devices, on_device(): lax.all_to_all(partial_value, 'dst', split_axis=0, concat_axis=0, tiled=T...  97.9 us
    all_gather x1, waiting for transfers between devices, on_device(): gathered = lax.all_gather(history, 'dst', axis=0, tiled=True)  59.7 us
    all_to_all x1, waiting for transfers between devices, on_device(): lax.all_to_all(lax.all_to_all(partial_value, 'dst', split_axis=0, concat_...  27.6 us
    unnamed x19, local copies, waits for them, and re-layouts  27.5 us
    all_to_all x1, starting transfers between devices, on_device(): lax.all_to_all(spread, 'dst', split_axis=0, concat_axis=0, tiled=True)  16.8 us
  transfers between devices with their start and end apart: 6, of which 4 were waited for; matrix products, arithmetic and copies ran while one was open for 8% of the time, Pallas kernels for 0%

commit v1 on v0

v1 whole, which is shorter than its diff:
```python
import jax
import jax.numpy as jnp
from jax import lax
from jax.experimental import pallas as pl
from jax.experimental.pallas import tpu as pltpu
from jax.sharding import PartitionSpec as P

MESH = pl.DeviceIdType.MESH
NZ, NC, NS = 16, 2, 16
NP = NC * NS
BLK, F, TPS, SLOTS, OWN, NJ = 64, 128, 8, 64, 16, 4
HZ = NZ // 2
LANES = 128
TREE = (
    (0, (3, -3, 1, -1)),
    (3, (3, -1, 1)),
    (-3, (-3, 1, -1)),
    (6, (2, 1, -1)),
    (-6, (-1, 1)),
    (1, ()),
    (-1, ()),
    (2, ()),
    (-2, ()),
    (4, ()),
    (-4, ()),
    (5, ()),
    (-5, ()),
    (7, ()),
    (-7, ()),
    (8, ()),
)
NEAR = (1, -1, 2, -2, 3, -3)
F32, BF16 = jnp.float32, jnp.bfloat16


def body(
    cols,
    adj_hbm,
    hist_hbm,
    ids_hbm,
    feats_hbm,
    cot_hbm,
    wn_hbm,
    ws_hbm,
    bias_hbm,
    emb_ref,
    gn_ref,
    gs_ref,
    gb_ref,
    adj,
    table,
    ids,
    feats,
    cot,
    wn,
    ws,
    bias,
    part,
    outbox,
    inbox,
    idbox,
    zout,
    zin,
    grad,
    gbias,
    gin,
    gbin,
    gsum,
    gbsum,
    gzin,
    gbzin,
    gfin,
    gall,
    load_sem,
    adj_sem,
    table_sem,
    table_in,
    pair_in,
    send_sem,
    in_sem,
    id_sem,
    z_sem,
    g_sem,
    gb_sem,
    gz_sem,
    gbz_sem,
    ga_sem,
):
    d = lax.axis_index("dst")
    s = lax.axis_index("src")
    z = d // NC
    c = d % NC
    me = c * NS + s

    def plane(i):
        return (z * NC + i // NS, i % NS)

    def at_z(t):
        return (t * NC + c, s)

    small = [
        pltpu.make_async_copy(a, b, load_sem.at[n])
        for n, (a, b) in enumerate(
            (
                (ids_hbm, ids),
                (feats_hbm, feats),
                (cot_hbm, cot),
                (wn_hbm, wn),
                (ws_hbm, ws),
                (bias_hbm, bias),
            )
        )
    ]
    own = pltpu.make_async_copy(hist_hbm, table.at[pl.ds(d * 2, 2)], table_sem)
    own.start()
    big = pltpu.make_async_copy(adj_hbm, adj, adj_sem)

    barrier = pltpu.get_barrier_semaphore()
    for off in NEAR:
        pl.semaphore_signal(
            barrier, inc=1, device_id=at_z((z + off + NZ) % NZ), device_id_type=MESH
        )

    def greet(k, carry):
        pl.semaphore_signal(
            barrier, inc=1, device_id=plane((me + k) % NP), device_id_type=MESH
        )
        return carry

    lax.fori_loop(1, NP, greet, 0)
    for op in small:
        op.start()
    big.start()
    own.wait()
    pl.semaphore_wait(barrier, NP - 1 + len(NEAR))

    slot_of = {off: n for n, (off, _) in enumerate(TREE)}

    def block(off):
        return table.at[pl.ds(((z - off + NZ) % NZ) * (2 * NC) + c * 2, 2)]

    def wire(off, step):
        landing = off + step
        return pltpu.make_async_remote_copy(
            src_ref=block(off),
            dst_ref=block(off),
            send_sem=send_sem.at[0],
            recv_sem=table_in.at[slot_of[landing]],
            device_id=at_z((z + step + NZ) % NZ),
            device_id_type=MESH,
        )

    def twin(off):
        return pltpu.make_async_remote_copy(
            src_ref=block(off),
            dst_ref=block(off),
            send_sem=send_sem.at[0],
            recv_sem=pair_in,
            device_id=(z * NC + 1 - c, s),
            device_id_type=MESH,
        )

    for off, moves in TREE:
        if off != 0:
            pltpu.make_async_copy(block(off), block(off), table_in.at[slot_of[off]]).wait()
        for step in moves:
            wire(off, step).start()
        twin(off).start()

    small[0].wait()

    def send_ids(k, carry):
        i = (me + k) % NP
        pltpu.make_async_remote_copy(
            src_ref=ids.at[i // NS],
            dst_ref=idbox.at[me],
            send_sem=send_sem.at[1],
            recv_sem=id_sem,
            device_id=plane(i),
            device_id_type=MESH,
        ).start()
        return carry

    lax.fori_loop(1, NP, send_ids, 0)
    pltpu.make_async_copy(ids.at[c], idbox.at[me], id_sem).start()

    big.wait()
    pltpu.make_async_copy(
        table.at[pl.ds(0, 2 * NZ)], table.at[pl.ds(0, 2 * NZ)], pair_in
    ).wait()

    for h in range(2):

        def slot(n, carry):
            q = (n // 4) * 8 + h * 4 + n % 4
            picked = jnp.concatenate([table[cols[q, t]] for t in range(TPS)], axis=0)
            part[n] = jnp.dot(adj[q], picked, preferred_element_type=F32)
            return carry

        lax.fori_loop(0, SLOTS // 2, slot, 0, unroll=4)

        def pack(i, carry):
            for j in range(NJ):
                row = (i % NS) * NJ + j
                two = [
                    part[pl.ds((i // NS) * 2 + k, HZ, stride=4), row, :] for k in range(2)
                ]
                outbox[h, i, j] = jnp.concatenate(two, axis=0).astype(BF16)
            return carry

        lax.fori_loop(0, NP, pack, 0)

        def send(k, carry):
            i = (me + k) % NP
            pltpu.make_async_remote_copy(
                src_ref=outbox.at[h, i],
                dst_ref=inbox.at[h, me],
                send_sem=send_sem.at[2],
                recv_sem=in_sem.at[h],
                device_id=plane(i),
                device_id_type=MESH,
            ).start()
            return carry

        lax.fori_loop(1, NP, send, 0)
        pltpu.make_async_copy(outbox.at[h, me], inbox.at[h, me], in_sem.at[h]).start()

    for op in small[1:]:
        op.wait()

    pltpu.make_async_copy(idbox, idbox, id_sem).wait()
    lane_dev = lax.broadcasted_iota(jnp.int32, (1, LANES), 1) // 16
    row_id = lax.broadcasted_iota(jnp.int32, (LANES, LANES), 0)
    for h in range(2):
        parts = []
        for g in range(NP // 8):
            row = jnp.zeros((1, LANES), jnp.int32)
            for n in range(8):
                row = jnp.where(lane_dev == n, idbox[g * 8 + n, pl.ds(h, 1), :], row)
            parts.append((row_id == row).astype(F32).astype(BF16))
        chosen = jnp.concatenate(parts, axis=1)
        pltpu.make_async_copy(inbox.at[h], inbox.at[h], in_sem.at[h]).wait()
        for j in range(NJ):
            got = inbox[h, :, j].reshape(NP * 16, F)
            total = jnp.dot(chosen, got, preferred_element_type=F32)
            zout[h, :, j] = total.astype(BF16).reshape(HZ, OWN, F)
        for i in range(HZ):
            t = 2 * i + h

            @pl.when(t != z)
            def _():
                pltpu.make_async_remote_copy(
                    src_ref=zout.at[h, i],
                    dst_ref=zin.at[z],
                    send_sem=send_sem.at[3],
                    recv_sem=z_sem,
                    device_id=at_z(t),
                    device_id_type=MESH,
                ).start()

            @pl.when(t == z)
            def _():
                pltpu.make_async_copy(zout.at[h, i], zin.at[z], z_sem).start()

    pltpu.make_async_copy(zin, zin, z_sem).wait()

    aggs, selfs, grads_low = [], [], []
    gbias_sum = jnp.zeros((1, F), F32)
    for j in range(NJ):
        agg = zin[0, j].astype(F32)
        for t in range(1, NZ):
            agg = agg + zin[t, j].astype(F32)
        agg = agg.astype(BF16)
        mine = feats[:, j * F : (j + 1) * F]
        pre = (
            jnp.dot(agg, wn[...], preferred_element_type=F32)
            + jnp.dot(mine, ws[...], preferred_element_type=F32)
            + bias[...]
        )
        sig = jax.nn.sigmoid(pre)
        emb_ref[:, j * F : (j + 1) * F] = (pre * sig).astype(BF16)
        slope = sig * (1.0 + pre * (1.0 - sig))
        gpre = cot[:, j * F : (j + 1) * F].astype(F32) * slope * (float(NZ * NC * OWN * BLK) ** -0.5)
        gbias_sum = gbias_sum + jnp.sum(gpre, axis=0, keepdims=True)
        aggs.append(agg)
        selfs.append(mine)
        grads_low.append(gpre.astype(BF16))
    low = jnp.concatenate(grads_low, axis=0)
    for n, left in enumerate((aggs, selfs)):
        left = jnp.concatenate(left, axis=0)
        prod = lax.dot_general(
            left, low, (((0,), (0,)), ((), ())), preferred_element_type=F32
        )
        grad[pl.ds(n * 16, 16)] = prod.reshape(16, 8, F)
    gbias[...] = gbias_sum

    def scatter(k, carry):
        i = (me + k) % NP
        pltpu.make_async_remote_copy(
            src_ref=grad.at[i],
            dst_ref=gin.at[me],
            send_sem=send_sem.at[4],
            recv_sem=g_sem,
            device_id=plane(i),
            device_id_type=MESH,
        ).start()
        pltpu.make_async_remote_copy(
            src_ref=gbias,
            dst_ref=gbin.at[me],
            send_sem=send_sem.at[5],
            recv_sem=gb_sem,
            device_id=plane(i),
            device_id_type=MESH,
        ).start()
        return carry

    lax.fori_loop(1, NP, scatter, 0)
    pltpu.make_async_copy(grad.at[me], gin.at[me], g_sem).start()
    pltpu.make_async_copy(gbias, gbin.at[me], gb_sem).start()
    pltpu.make_async_copy(gin, gin, g_sem).wait()
    pltpu.make_async_copy(gbin, gbin, gb_sem).wait()
    total, btotal = gin[0], gbin[0]
    for i in range(1, NP):
        total = total + gin[i]
        btotal = btotal + gbin[i]
    gsum[...] = total
    gbsum[...] = btotal

    def along(k, carry):
        t = (z + k) % NZ
        pltpu.make_async_remote_copy(
            src_ref=gsum,
            dst_ref=gzin.at[z],
            send_sem=send_sem.at[6],
            recv_sem=gz_sem,
            device_id=at_z(t),
            device_id_type=MESH,
        ).start()
        pltpu.make_async_remote_copy(
            src_ref=gbsum,
            dst_ref=gbzin.at[z],
            send_sem=send_sem.at[7],
            recv_sem=gbz_sem,
            device_id=at_z(t),
            device_id_type=MESH,
        ).start()
        return carry

    lax.fori_loop(1, NZ, along, 0)
    pltpu.make_async_copy(gsum, gzin.at[z], gz_sem).start()
    pltpu.make_async_copy(gbsum, gbzin.at[z], gbz_sem).start()
    pltpu.make_async_copy(gzin, gzin, gz_sem).wait()
    pltpu.make_async_copy(gbzin, gbzin, gbz_sem).wait()
    total, btotal = gzin[0], gbzin[0]
    for t in range(1, NZ):
        total = total + gzin[t]
        btotal = btotal + gbzin[t]
    gfin[...] = total
    gb_ref[...] = btotal

    def gather(k, carry):
        pltpu.make_async_remote_copy(
            src_ref=gfin,
            dst_ref=gall.at[me],
            send_sem=send_sem.at[8],
            recv_sem=ga_sem,
            device_id=plane((me + k) % NP),
            device_id_type=MESH,
        ).start()
        return carry

    lax.fori_loop(1, NP, gather, 0)
    pltpu.make_async_copy(gfin, gall.at[me], ga_sem).start()
    pltpu.make_async_copy(gall, gall, ga_sem).wait()
    gn_ref[...] = gall[pl.ds(0, 16)].reshape(F, F)
    gs_ref[...] = gall[pl.ds(16, 16)].reshape(F, F)

    def sent(n, ref):
        pltpu.make_async_copy(ref, ref, send_sem.at[n]).wait()

    sent(0, table.at[pl.ds(0, 2 * (2 * NZ - 1))])
    sent(1, idbox.at[pl.ds(0, NP - 1)])
    for _ in range(2):
        sent(2, inbox.at[0, pl.ds(0, NP - 1)])
    sent(3, zin.at[pl.ds(0, NZ - 1)])
    sent(4, gin.at[pl.ds(0, NP - 1)])
    sent(5, gbin.at[pl.ds(0, NP - 1)])
    sent(6, gzin.at[pl.ds(0, NZ - 1)])
    sent(7, gbzin.at[pl.ds(0, NZ - 1)])
    sent(8, gall.at[pl.ds(0, NP - 1)])


def on_device(
    adj_tiles,
    tile_cols,
    send_block,
    send_count,
    history,
    node_feats,
    w_neigh,
    w_self,
    out_bias,
    cotangent,
):
    adj = adj_tiles.reshape(SLOTS, BLK, TPS * BLK)
    cols = tile_cols.reshape(SLOTS, TPS)
    hist = history.reshape(2, BLK, F)
    count = send_count.reshape(HZ, 2, NC, 1)
    dest = send_block.reshape(HZ, 2, NC, 2)
    alive = jnp.arange(2)[None, None, None, :] < count
    ids = jnp.where(alive, dest + jnp.arange(HZ)[:, None, None, None] * OWN, -1)
    ids = ids.transpose(2, 1, 3, 0).reshape(NC, 2, 16)
    ids = jnp.tile(ids, (1, 1, LANES // 16))
    any_spec = pl.BlockSpec(memory_space=pl.ANY)
    vmem_spec = pl.BlockSpec(memory_space=pltpu.VMEM)
    dma = pltpu.SemaphoreType.DMA
    emb, gn, gs, gb = pl.pallas_call(
        body,
        out_shape=(
            jax.ShapeDtypeStruct(node_feats.shape, BF16),
            jax.ShapeDtypeStruct((F, F), F32),
            jax.ShapeDtypeStruct((F, F), F32),
            jax.ShapeDtypeStruct((1, F), F32),
        ),
        in_specs=[pl.BlockSpec(memory_space=pltpu.SMEM)] + [any_spec] * 8,
        out_specs=(vmem_spec,) * 4,
        scratch_shapes=[
            pltpu.VMEM((SLOTS, BLK, TPS * BLK), BF16),
            pltpu.VMEM((2 * NC * NZ, BLK, F), BF16),
            pltpu.VMEM((NC, 2, LANES), jnp.int32),
            pltpu.VMEM(node_feats.shape, BF16),
            pltpu.VMEM(node_feats.shape, BF16),
            pltpu.VMEM((F, F), BF16),
            pltpu.VMEM((F, F), BF16),
            pltpu.VMEM((1, F), F32),
            pltpu.VMEM((SLOTS // 2, BLK, F), F32),
            pltpu.VMEM((2, NP, NJ, 16, F), BF16),
            pltpu.VMEM((2, NP, NJ, 16, F), BF16),
            pltpu.VMEM((NP, 2, LANES), jnp.int32),
            pltpu.VMEM((2, HZ, NJ, OWN, F), BF16),
            pltpu.VMEM((NZ, NJ, OWN, F), BF16),
            pltpu.VMEM((NP, 8, F), F32),
            pltpu.VMEM((1, F), F32),
            pltpu.VMEM((NP, 8, F), F32),
            pltpu.VMEM((NP, 1, F), F32),
            pltpu.VMEM((8, F), F32),
            pltpu.VMEM((1, F), F32),
            pltpu.VMEM((NZ, 8, F), F32),
            pltpu.VMEM((NZ, 1, F), F32),
            pltpu.VMEM((8, F), F32),
            pltpu.VMEM((NP, 8, F), F32),
            dma((6,)),
            dma,
            dma,
            dma((NZ,)),
            dma,
            dma((9,)),
            dma((2,)),
            dma,
            dma,
            dma,
            dma,
            dma,
            dma,
            dma,
        ],
        compiler_params=pltpu.CompilerParams(collective_id=0, has_side_effects=True),
    )(
        cols,
        adj,
        hist,
        ids,
        node_feats,
        cotangent,
        w_neigh,
        w_self,
        out_bias.reshape(1, F),
    )
    return emb, gn, gs, gb.reshape(F)


def solution(mesh):
    in_specs = (
        P("dst", "src", None, None, None),
        P("dst", "src", None, None),
        P("dst", "src", None, None),
        P("dst", "src", None),
        P("dst", "src", None),
        P("dst", "src"),
        P(),
        P(),
        P(),
        P("dst", "src"),
    )
    out_specs = (P("dst", "src"), P(), P(), P())
    return jax.shard_map(
        on_device, mesh=mesh, in_specs=in_specs, out_specs=out_specs, check_vma=False
    )
```

time: 782 us -> 93.3 us (0.12)
  waiting for transfers between devices: 525 us -> 0 us
  blocking collectives: 104 us -> 0 us
  Pallas kernels: 0 us -> 80.4 us
  local copies, waits for them, and re-layouts: 68.5 us -> 10.3 us
  starting transfers between devices: 38.3 us -> 0 us
  other arithmetic: 20.1 us -> 1.4 us
  between operations: 14.2 us -> 0.66 us
  matrix products: 10.7 us -> 0 us
    psum x1 -> x0, waiting for transfers between devices: 340 us -> none  [on_device(): lax.psum((grad_neigh, grad_self, grad_bias), ('dst', 'src'))]
    all_to_all x4 -> x0, waiting for transfers between devices: 126 us -> none  [the longest x1 97.9 us: on_device(): lax.all_to_all(partial_value, 'dst', split_axis=0, concat_axis=0, tiled=T...]
    psum x1 -> x0, blocking collectives: 104 us -> none  [on_device(): lax.psum((grad_neigh, grad_self, grad_bias), ('dst', 'src'))]
    pallas_call x0 -> x1, Pallas kernels: none -> 80.4 us  [on_device(): pl.pallas_call(body, out_shape=(jax.ShapeDtypeStruct(node_feats.shape, BF...]
    all_gather x1 -> x0, waiting for transfers between devices: 59.7 us -> none  [on_device(): gathered = lax.all_gather(history, 'dst', axis=0, tiled=True)]
    all_to_all x4 -> x0, starting transfers between devices: 38.2 us -> none  [the longest x1 16.8 us: on_device(): lax.all_to_all(spread, 'dst', split_axis=0, concat_axis=0, tiled=True)]
    all_to_all x5 -> x0, local copies, waits for them, and re-layouts: 20.3 us -> none  [the longest x2 10.9 us: on_device(): lax.all_to_all(lax.all_to_all(partial_value, 'dst', split_axis=0, concat_...]
    unnamed x19 -> x7, local copies, waits for them, and re-layouts: 27.5 us -> 8.72 us
  transfers between devices with their start and end apart: 6 -> 0, of which waited for: 4 -> 0; matrix products, arithmetic and copies ran while one was open for 8% -> 0% of each run, Pallas kernels for 0% -> 0%
where the time goes in v1:
time: 93.3 us; the launch traced here: 92.8 us
  Pallas kernels  80.4 us (86%)
  local copies, waits for them, and re-layouts  10.3 us (11%)
  other arithmetic  1.4 us (2%)
    pallas_call x1, Pallas kernels, on_device(): pl.pallas_call(body, out_shape=(jax.ShapeDtypeStruct(node_feats.shape, BF...  80.4 us
    unnamed x7, local copies, waits for them, and re-layouts  8.72 us

profile of v1, /device:TPU:1, one launch (start us, length us, event | category | flops | bytes accessed | tf_op | source)
XLA Modules:
  0.0 92.8 jit_solution(8855986098423096485)
XLA Ops:
  0.6 0.5 broadcast.15
  1.1 1.3 %reduce.3 = s32[32]{0:T(128)S(1)} reduce(s32[1,1,32]{2,1,0:T(1,128)} %param.13, s32[]{:T(128)} %broadcast.15), dimensions={0,1}, to_apply=%param.13.reduce_sub_computation.3 | reduce | bytes 260 | tf_op args[3]
  2.5 0.1 lt.16
  2.6 0.8 reshape.40
  3.3 0.1 compare_select_fusion
  3.4 0.1 copy.18
  3.5 0.7 tile.12.ids_hbm
  4.2 1.4 %copy.16 = s32[1,1,64,8]{3,2,1,0:T(8,128)} copy(s32[1,1,64,8]{2,3,1,0:T(8,128)} %param.11) | data formatting | bytes 4096 | tf_op args[1]
  5.6 1.4 %copy.21 = bf16[1,2,64,128]{3,2,1,0:T(8,128)(2,1)} copy(bf16[1,2,64,128]{3,1,2,0:T(2,128)(2,1)} %bitcast.21) | data formatting | bytes 65536
  6.9 80.4 %shard_map.129 = (bf16[16,512]{1,0:T(8,128)(2,1)}, f32[128,128]{1,0:T(8,128)}, f32[128,128]{1,0:T(8,128)}, f32[1,128]{1,0:T(1,128)}) custom-call(s32[64,8]{1,0:T(8,128)} %bitcast.18, bf16[64,64,512]{2,1,0:T(8,128)(2,1)} %bitcast.17, bf16[2,64,128]{2,1,0:T(8,128)(2,1)} %bitcast.19, s32[2,2,128]{2,1,0:T(2,128)} %tile.12.ids_hbm, bf16[16,512]{1,0:T(8,128)(2,1)} %feats_hbm.1, ...), custom_call_target="tpu_custom_call" | custom-call | tf_op jit(solution)/shard_map/pallas_call | solution.py:417
  87.4 1.3 %copy.26 = bf16[16,512]{1,0:T(8,128)(2,1)} copy(bf16[16,512]{1,0:T(8,128)(2,1)} %get-tuple-element.16) | data formatting | bytes 32768
  88.7 1.5 %copy.27 = f32[128,128]{1,0:T(8,128)} copy(f32[128,128]{1,0:T(8,128)} %get-tuple-element.17) | data formatting | bytes 131072
  90.2 1.5 %copy.28 = f32[128,128]{1,0:T(8,128)} copy(f32[128,128]{1,0:T(8,128)} %get-tuple-element.18) | data formatting | bytes 131072
  91.6 1.2 %copy.29 = f32[128]{0:T(128)} copy(f32[128]{0:T(128)} %bitcast.23) | data formatting | bytes 1024
  (2 shorter events, 0.0 us)

commit v2 on v1

--- a/solution.py
+++ b/solution.py
@@ -34,20 +34,24 @@
 
 
 def body(
-    cols,
+    cols_hbm,
+    block_hbm,
+    count_hbm,
     adj_hbm,
     hist_hbm,
-    ids_hbm,
     feats_hbm,
     cot_hbm,
     wn_hbm,
     ws_hbm,
     bias_hbm,
     emb_ref,
-    gn_ref,
-    gs_ref,
+    grads_ref,
     gb_ref,
+    cols,
+    blocks,
+    counts,
     adj,
+    hist,
     table,
     ids,
     feats,
@@ -102,7 +106,9 @@
         pltpu.make_async_copy(a, b, load_sem.at[n])
         for n, (a, b) in enumerate(
             (
-                (ids_hbm, ids),
+                (cols_hbm, cols),
+                (block_hbm, blocks),
+                (count_hbm, counts),
                 (feats_hbm, feats),
                 (cot_hbm, cot),
                 (wn_hbm, wn),
@@ -111,7 +117,7 @@
             )
         )
     ]
-    own = pltpu.make_async_copy(hist_hbm, table.at[pl.ds(d * 2, 2)], table_sem)
+    own = pltpu.make_async_copy(hist_hbm, hist, table_sem)
     own.start()
     big = pltpu.make_async_copy(adj_hbm, adj, adj_sem)
 
@@ -132,6 +138,20 @@
         op.start()
     big.start()
     own.wait()
+    for g in range(2):
+        table[d * 2 + g] = hist[:, g, :]
+    for op in small[:3]:
+        op.wait()
+    lane_slot = lax.broadcasted_iota(jnp.int32, (1, LANES), 1) % 16
+    for core in range(NC):
+        for h in range(2):
+            row = jnp.full((1, LANES), -1, jnp.int32)
+            for n in range(16):
+                k, i = n // HZ, n % HZ
+                p = (2 * i + h) * NC + core
+                value = jnp.where(counts[0, p] > k, blocks[k, p] + i * OWN, -1)
+                row = jnp.where(lane_slot == n, value, row)
+            ids[core, pl.ds(h, 1), :] = row
     pl.semaphore_wait(barrier, NP - 1 + len(NEAR))
 
     slot_of = {off: n for n, (off, _) in enumerate(TREE)}
@@ -167,8 +187,6 @@
             wire(off, step).start()
         twin(off).start()
 
-    small[0].wait()
-
     def send_ids(k, carry):
         i = (me + k) % NP
         pltpu.make_async_remote_copy(
@@ -193,7 +211,7 @@
 
         def slot(n, carry):
             q = (n // 4) * 8 + h * 4 + n % 4
-            picked = jnp.concatenate([table[cols[q, t]] for t in range(TPS)], axis=0)
+            picked = jnp.concatenate([table[cols[t, q]] for t in range(TPS)], axis=0)
             part[n] = jnp.dot(adj[q], picked, preferred_element_type=F32)
             return carry
 
@@ -225,7 +243,7 @@
         lax.fori_loop(1, NP, send, 0)
         pltpu.make_async_copy(outbox.at[h, me], inbox.at[h, me], in_sem.at[h]).start()
 
-    for op in small[1:]:
+    for op in small[3:]:
         op.wait()
 
     pltpu.make_async_copy(idbox, idbox, id_sem).wait()
@@ -372,8 +390,7 @@
     lax.fori_loop(1, NP, gather, 0)
     pltpu.make_async_copy(gfin, gall.at[me], ga_sem).start()
     pltpu.make_async_copy(gall, gall, ga_sem).wait()
-    gn_ref[...] = gall[pl.ds(0, 16)].reshape(F, F)
-    gs_ref[...] = gall[pl.ds(16, 16)].reshape(F, F)
+    grads_ref[...] = gall[...]
 
     def sent(n, ref):
         pltpu.make_async_copy(ref, ref, send_sem.at[n]).wait()
@@ -388,6 +405,13 @@
     sent(6, gzin.at[pl.ds(0, NZ - 1)])
     sent(7, gbzin.at[pl.ds(0, NZ - 1)])
     sent(8, gall.at[pl.ds(0, NP - 1)])
+
+
+def hand_over(emb_ref, grads_ref, gb_ref, emb_out, gn_out, gs_out, gb_out):
+    emb_out[...] = emb_ref[...]
+    gn_out[...] = grads_ref[pl.ds(0, 16)].reshape(F, F)
+    gs_out[...] = grads_ref[pl.ds(16, 16)].reshape(F, F)
+    gb_out[...] = gb_ref[0]
 
 
 def on_device(
@@ -403,29 +427,28 @@
     cotangent,
 ):
     adj = adj_tiles.reshape(SLOTS, BLK, TPS * BLK)
-    cols = tile_cols.reshape(SLOTS, TPS)
-    hist = history.reshape(2, BLK, F)
-    count = send_count.reshape(HZ, 2, NC, 1)
-    dest = send_block.reshape(HZ, 2, NC, 2)
-    alive = jnp.arange(2)[None, None, None, :] < count
-    ids = jnp.where(alive, dest + jnp.arange(HZ)[:, None, None, None] * OWN, -1)
-    ids = ids.transpose(2, 1, 3, 0).reshape(NC, 2, 16)
-    ids = jnp.tile(ids, (1, 1, LANES // 16))
+    cols = tile_cols.reshape(SLOTS, TPS).T
+    block = send_block.reshape(NP, 2).T
+    count = send_count.reshape(1, NP)
+    hist = history.reshape(2, BLK, F).transpose(1, 0, 2)
     any_spec = pl.BlockSpec(memory_space=pl.ANY)
     vmem_spec = pl.BlockSpec(memory_space=pltpu.VMEM)
     dma = pltpu.SemaphoreType.DMA
-    emb, gn, gs, gb = pl.pallas_call(
+    emb, grads, gb = pl.pallas_call(
         body,
         out_shape=(
             jax.ShapeDtypeStruct(node_feats.shape, BF16),
-            jax.ShapeDtypeStruct((F, F), F32),
-            jax.ShapeDtypeStruct((F, F), F32),
+            jax.ShapeDtypeStruct((NP, 8, F), F32),
             jax.ShapeDtypeStruct((1, F), F32),
         ),
-        in_specs=[pl.BlockSpec(memory_space=pltpu.SMEM)] + [any_spec] * 8,
-        out_specs=(vmem_spec,) * 4,
+        in_specs=[any_spec] * 10,
+        out_specs=(vmem_spec,) * 3,
         scratch_shapes=[
+            pltpu.SMEM((TPS, SLOTS), jnp.int32),
+            pltpu.SMEM((2, NP), jnp.int32),
+            pltpu.SMEM((1, NP), jnp.int32),
             pltpu.VMEM((SLOTS, BLK, TPS * BLK), BF16),
+            pltpu.VMEM((BLK, 2, F), BF16),
             pltpu.VMEM((2 * NC * NZ, BLK, F), BF16),
             pltpu.VMEM((NC, 2, LANES), jnp.int32),
             pltpu.VMEM(node_feats.shape, BF16),
@@ -449,7 +472,7 @@
             pltpu.VMEM((NZ, 1, F), F32),
             pltpu.VMEM((8, F), F32),
             pltpu.VMEM((NP, 8, F), F32),
-            dma((6,)),
+            dma((8,)),
             dma,
             dma,
             dma((NZ,)),
@@ -467,16 +490,27 @@
         compiler_params=pltpu.CompilerParams(collective_id=0, has_side_effects=True),
     )(
         cols,
+        block,
+        count,
         adj,
         hist,
-        ids,
         node_feats,
         cotangent,
         w_neigh,
         w_self,
         out_bias.reshape(1, F),
     )
-    return emb, gn, gs, gb.reshape(F)
+    return pl.pallas_call(
+        hand_over,
+        out_shape=(
+            jax.ShapeDtypeStruct(node_feats.shape, BF16),
+            jax.ShapeDtypeStruct((F, F), F32),
+            jax.ShapeDtypeStruct((F, F), F32),
+            jax.ShapeDtypeStruct((F,), F32),
+        ),
+        in_specs=[vmem_spec] * 3,
+        out_specs=(vmem_spec,) * 4,
+    )(emb, grads, gb)
 
 
 def solution(mesh):

time: 93.3 us -> 81.7 us (0.88)
  local copies, waits for them, and re-layouts: 10.3 us -> 0 us
  other arithmetic: 1.4 us -> 0 us
    unnamed x7 -> x0, local copies, waits for them, and re-layouts: 8.72 us -> none
    pallas_call x0 -> x1, Pallas kernels: none -> 1.57 us  [on_device(): pl.pallas_call(hand_over, out_shape=(jax.ShapeDtypeStruct(node_feats.shap...]
    unnamed x1 -> x0, other arithmetic: 1.32 us -> none
    pallas_call x1, Pallas kernels: 80.4 us -> 79.3 us  [on_device(): pl.pallas_call(body, out_shape=(jax.ShapeDtypeStruct(node_feats.shape, BF...]
where the time goes in v2:
time: 81.7 us; the launch traced here: 81.5 us
  Pallas kernels  80.9 us (99%)
    pallas_call x1, Pallas kernels, on_device(): pl.pallas_call(body, out_shape=(jax.ShapeDtypeStruct(node_feats.shape, BF...  79.3 us

profile of v2, /device:TPU:1, one launch (start us, length us, event | category | flops | bytes accessed | tf_op | source)
XLA Modules:
  0.0 81.5 jit_solution(3961968917120270636)
XLA Ops:
  0.6 79.3 %shard_map.129 = (bf16[16,512]{1,0:T(8,128)(2,1)}, f32[32,8,128]{2,1,0:T(8,128)}, f32[1,128]{1,0:T(1,128)}) custom-call(s32[8,64]{1,0:T(8,128)} %bitcast.14, s32[2,32]{1,0:T(2,128)} %bitcast.15, s32[1,32]{1,0:T(1,128)} %bitcast.16, bf16[64,64,512]{2,1,0:T(8,128)(2,1)} %bitcast.12, bf16[64,2,128]{2,1,0:T(2,128)(2,1)} %bitcast.13, bf16[16,512]{1,0:T(8,128)(2,1)} %feats_hbm.1, ...), custom_call_target="tpu_custom_call" | custom-call | tf_op jit(solution)/shard_map/pallas_call | solution.py:437
  80.0 1.6 %shard_map.130 = (bf16[16,512]{1,0:T(8,128)(2,1)}, f32[128,128]{1,0:T(8,128)}, f32[128,128]{1,0:T(8,128)}, f32[128]{0:T(128)}) custom-call(bf16[16,512]{1,0:T(8,128)(2,1)} %get-tuple-element.7.emb_ref, f32[32,8,128]{2,1,0:T(8,128)} %get-tuple-element.8.grads_ref, f32[1,128]{1,0:T(1,128)} %get-tuple-element.9.gb_ref), custom_call_target="tpu_custom_call" | custom-call | tf_op jit(solution)/shard_map/pallas_call | solution.py:503

commit v3 on v2

--- a/solution.py
+++ b/solution.py
@@ -29,6 +29,10 @@
     (-7, ()),
     (8, ()),
 )
+LEVELS = ((0,), (3, -3), (6, -6), (1, -1, 2, -2, 4, -4, 5, -5, 7, -7, 8))
+PIECE = 16
+FIRST = (4, 12)
+SEND_ORDER = ((4, 3, 5, 2, 6, 1, 7, 0), (0, 1, 7, 2, 6, 3, 5, 4))
 NEAR = (1, -1, 2, -2, 3, -3)
 F32, BF16 = jnp.float32, jnp.bfloat16
 
@@ -102,6 +106,9 @@
     def at_z(t):
         return (t * NC + c, s)
 
+    def owner(h, i):
+        return (z + FIRST[h] + i) % NZ
+
     small = [
         pltpu.make_async_copy(a, b, load_sem.at[n])
         for n, (a, b) in enumerate(
@@ -148,7 +155,7 @@
             row = jnp.full((1, LANES), -1, jnp.int32)
             for n in range(16):
                 k, i = n // HZ, n % HZ
-                p = (2 * i + h) * NC + core
+                p = owner(h, i) * NC + core
                 value = jnp.where(counts[0, p] > k, blocks[k, p] + i * OWN, -1)
                 row = jnp.where(lane_slot == n, value, row)
             ids[core, pl.ds(h, 1), :] = row
@@ -156,36 +163,36 @@
 
     slot_of = {off: n for n, (off, _) in enumerate(TREE)}
 
-    def block(off):
-        return table.at[pl.ds(((z - off + NZ) % NZ) * (2 * NC) + c * 2, 2)]
-
-    def wire(off, step):
-        landing = off + step
-        return pltpu.make_async_remote_copy(
-            src_ref=block(off),
-            dst_ref=block(off),
+    def block(off, p):
+        first = ((z - off + NZ) % NZ) * (2 * NC) + c * 2
+        return table.at[pl.ds(first, 2), pl.ds(p * PIECE, PIECE)]
+
+    def push(off, p, sem, device):
+        pltpu.make_async_remote_copy(
+            src_ref=block(off, p),
+            dst_ref=block(off, p),
             send_sem=send_sem.at[0],
-            recv_sem=table_in.at[slot_of[landing]],
-            device_id=at_z((z + step + NZ) % NZ),
-            device_id_type=MESH,
-        )
-
-    def twin(off):
-        return pltpu.make_async_remote_copy(
-            src_ref=block(off),
-            dst_ref=block(off),
-            send_sem=send_sem.at[0],
-            recv_sem=pair_in,
-            device_id=(z * NC + 1 - c, s),
-            device_id_type=MESH,
-        )
-
-    for off, moves in TREE:
-        if off != 0:
-            pltpu.make_async_copy(block(off), block(off), table_in.at[slot_of[off]]).wait()
-        for step in moves:
-            wire(off, step).start()
-        twin(off).start()
+            recv_sem=sem,
+            device_id=device,
+            device_id_type=MESH,
+        ).start()
+
+    moves = dict(TREE)
+    for level in LEVELS:
+        for p in range(BLK // PIECE):
+            for off in level:
+                if off != 0:
+                    pltpu.make_async_copy(
+                        block(off, p), block(off, p), table_in.at[slot_of[off], p]
+                    ).wait()
+                for step in moves[off]:
+                    push(
+                        off,
+                        p,
+                        table_in.at[slot_of[off + step], p],
+                        at_z((z + step + NZ) % NZ),
+                    )
+                push(off, p, pair_in, (z * NC + 1 - c, s))
 
     def send_ids(k, carry):
         i = (me + k) % NP
@@ -210,7 +217,7 @@
     for h in range(2):
 
         def slot(n, carry):
-            q = (n // 4) * 8 + h * 4 + n % 4
+            q = owner(h, n // 4) * 4 + n % 4
             picked = jnp.concatenate([table[cols[t, q]] for t in range(TPS)], axis=0)
             part[n] = jnp.dot(adj[q], picked, preferred_element_type=F32)
             return carry
@@ -262,23 +269,18 @@
             got = inbox[h, :, j].reshape(NP * 16, F)
             total = jnp.dot(chosen, got, preferred_element_type=F32)
             zout[h, :, j] = total.astype(BF16).reshape(HZ, OWN, F)
-        for i in range(HZ):
-            t = 2 * i + h
-
-            @pl.when(t != z)
-            def _():
+        for i in SEND_ORDER[h]:
+            if FIRST[h] + i == NZ:
+                pltpu.make_async_copy(zout.at[h, i], zin.at[z], z_sem).start()
+            else:
                 pltpu.make_async_remote_copy(
                     src_ref=zout.at[h, i],
                     dst_ref=zin.at[z],
                     send_sem=send_sem.at[3],
                     recv_sem=z_sem,
-                    device_id=at_z(t),
+                    device_id=at_z(owner(h, i)),
                     device_id_type=MESH,
                 ).start()
-
-            @pl.when(t == z)
-            def _():
-                pltpu.make_async_copy(zout.at[h, i], zin.at[z], z_sem).start()
 
     pltpu.make_async_copy(zin, zin, z_sem).wait()
 
@@ -344,8 +346,8 @@
     gsum[...] = total
     gbsum[...] = btotal
 
-    def along(k, carry):
-        t = (z + k) % NZ
+    def along(n, carry):
+        t = (z + HZ + (1 - 2 * (n % 2)) * ((n + 1) // 2) + NZ) % NZ
         pltpu.make_async_remote_copy(
             src_ref=gsum,
             dst_ref=gzin.at[z],
@@ -364,7 +366,7 @@
         ).start()
         return carry
 
-    lax.fori_loop(1, NZ, along, 0)
+    lax.fori_loop(0, NZ - 1, along, 0)
     pltpu.make_async_copy(gsum, gzin.at[z], gz_sem).start()
     pltpu.make_async_copy(gbsum, gbzin.at[z], gbz_sem).start()
     pltpu.make_async_copy(gzin, gzin, gz_sem).wait()
@@ -437,9 +439,9 @@
     emb, grads, gb = pl.pallas_call(
         body,
         out_shape=(
-            jax.ShapeDtypeStruct(node_feats.shape, BF16),
-            jax.ShapeDtypeStruct((NP, 8, F), F32),
-            jax.ShapeDtypeStruct((1, F), F32),
+            pltpu.VMEM(node_feats.shape, BF16),
+            pltpu.VMEM((NP, 8, F), F32),
+            pltpu.VMEM((1, F), F32),
         ),
         in_specs=[any_spec] * 10,
         out_specs=(vmem_spec,) * 3,
@@ -475,7 +477,7 @@
             dma((8,)),
             dma,
             dma,
-            dma((NZ,)),
+            dma((NZ, BLK // PIECE)),
             dma,
             dma((9,)),
             dma((2,)),
@@ -510,7 +512,7 @@
         ),
         in_specs=[vmem_spec] * 3,
         out_specs=(vmem_spec,) * 4,
-    )(emb, grads, gb)
+    )(*[pltpu.with_memory_space_constraint(x, pltpu.VMEM) for x in (emb, grads, gb)])
 
 
 def solution(mesh):

time: 81.7 us -> 76.9 us (0.941)
  Pallas kernels: 80.9 us -> 76.1 us
    pallas_call x1, Pallas kernels: 79.3 us -> 75.5 us  [on_device(): pl.pallas_call(body, out_shape=(pltpu.VMEM(node_feats.shape, BF16), pltpu...]
    pallas_call x1, Pallas kernels: 1.57 us -> 0.67 us  [on_device(): pl.pallas_call(hand_over, out_shape=(jax.ShapeDtypeStruct(node_feats.shap...]
where the time goes in v3:
time: 76.9 us; the launch traced here: 76.8 us
  Pallas kernels  76.1 us (99%)
    pallas_call x1, Pallas kernels, on_device(): pl.pallas_call(body, out_shape=(pltpu.VMEM(node_feats.shape, BF16), pltpu...  75.5 us

profile of v3, /device:TPU:1, one launch (start us, length us, event | category | flops | bytes accessed | tf_op | source)
XLA Modules:
  0.0 76.8 jit_solution(12199467713401751501)
XLA Ops:
  0.6 75.5 %shard_map.129 = (bf16[16,512]{1,0:T(8,128)(2,1)S(1)}, f32[32,8,128]{2,1,0:T(8,128)S(1)}, f32[1,128]{1,0:T(1,128)S(1)}) custom-call(s32[8,64]{1,0:T(8,128)} %bitcast.14, s32[2,32]{1,0:T(2,128)} %bitcast.15, s32[1,32]{1,0:T(1,128)} %bitcast.16, bf16[64,64,512]{2,1,0:T(8,128)(2,1)} %bitcast.12, bf16[64,2,128]{2,1,0:T(2,128)(2,1)} %bitcast.13, ...), custom_call_target="tpu_custom_call" | custom-call | tf_op jit(solution)/shard_map/pallas_call | solution.py:439
  76.1 0.7 shard_map.130
